TPU v7x, 32 devices: a whole 2x2x4 slice. The times are simulated.
32 devices in a mesh: dp: 4 (over y, x), tensor: 8 (over z, core).
Axes of the slice: x: 2, y: 2, z: 4, core: 2. Of those that a mesh axis runs over, the one named last changes fastest.
Arguments:
- block_in: bfloat16 [8192, 1024], P(('dp', 'tensor')), may hold values from -10 to 10
- cotangent: bfloat16 [8192, 1024], P(('dp', 'tensor')), may hold values from -6 to 6
- lengths: int32 [16], P('dp'), may hold values from 1 to 512, as said below
- qkv_weight: float32 [3, 1024, 1024], P(None, 'dp', 'tensor'), may hold values from -0.1875 to 0.1875
- proj_weight: float32 [1024, 1024], P('tensor', 'dp'), may hold values from -0.75 to 0.75
- expand_weight: float32 [1024, 4096], P('dp', 'tensor'), may hold values from -0.1875 to 0.1875
- reduce_weight: float32 [4096, 1024], P('tensor', 'dp'), may hold values from -0.09375 to 0.09375
- split_bias: float32 [16, 384], P('tensor', 'dp'), may hold values from -0.6 to 0.6
- vector_params: float32 [6, 1024], P(None, 'dp'), may hold values from -0.6 to 0.6
- qkv_moments: float32 [2, 3, 1024, 1024], P(None, None, 'dp', 'tensor'), may hold values from -3 to 3, as said below
- proj_moments: float32 [2, 1024, 1024], P(None, 'tensor', 'dp'), may hold values from -3 to 3, as said below
- expand_moments: float32 [2, 1024, 4096], P(None, 'dp', 'tensor'), may hold values from -3 to 3, as said below
- reduce_moments: float32 [2, 4096, 1024], P(None, 'tensor', 'dp'), may hold values from -3 to 3, as said below
- bias_moments: float32 [2, 16, 384], P(None, 'tensor', 'dp'), may hold values from -3 to 3, as said below
- vector_moments: float32 [2, 6, 1024], P(None, None, 'dp'), may hold values from -3 to 3, as said below
Outputs:
- block_out: bfloat16 [8192, 1024], P(('dp', 'tensor'))
- input_grad: bfloat16 [8192, 1024], P(('dp', 'tensor'))
- qkv_grad: float32 [3, 1024, 1024], P(None, 'dp', 'tensor')
- proj_grad: float32 [1024, 1024], P('tensor', 'dp')
- expand_grad: float32 [1024, 4096], P('dp', 'tensor')
- reduce_grad: float32 [4096, 1024], P('tensor', 'dp')
- bias_grad: float32 [16, 384], P('tensor', 'dp')
- vector_grad: float32 [6, 1024], P(None, 'dp')
- qkv_new: float32 [3, 1024, 1024], P(None, 'dp', 'tensor')
- proj_new: float32 [1024, 1024], P('tensor', 'dp')
- expand_new: float32 [1024, 4096], P('dp', 'tensor')
- reduce_new: float32 [4096, 1024], P('tensor', 'dp')
- bias_new: float32 [16, 384], P('tensor', 'dp')
- vector_new: float32 [6, 1024], P(None, 'dp')
- qkv_state: float32 [2, 3, 1024, 1024], P(None, None, 'dp', 'tensor')
- proj_state: float32 [2, 1024, 1024], P(None, 'tensor', 'dp')
- expand_state: float32 [2, 1024, 4096], P(None, 'dp', 'tensor')
- reduce_state: float32 [2, 4096, 1024], P(None, 'tensor', 'dp')
- bias_state: float32 [2, 16, 384], P(None, 'tensor', 'dp')
- vector_state: float32 [2, 6, 1024], P(None, None, 'dp')
Inputs may be any that keep to these rules, and one draw needn't show every extreme that they name: `lengths`: sequence s lies on the dp member s // (number of sequences per dp member); every draw has a sequence of exactly 512 live slots. `qkv_moments`: index 0 holds first moments, index 1 second moments of at least 0.01. `proj_moments`: index 0 holds first moments, index 1 second moments of at least 0.01. `expand_moments`: index 0 holds first moments, index 1 second moments of at least 0.01. `reduce_moments`: index 0 holds first moments, index 1 second moments of at least 0.01. `bias_moments`: index 0 holds first moments, index 1 second moments of at least 0.01. `vector_moments`: index 0 holds first moments, index 1 second moments of at least 0.01.
All inputs are finite; a program needn't handle non-finite values.
Results may differ from a plain program's by a relative error of at most 0.025.
Values may be sent and summed in bfloat16 or wider, within the bound.
No kernel may reach another device: no remote copies, remote signals or barrier semaphores. Data moves between devices by JAX's collectives and lax.ppermute only.
A program may use at most 192 MiB of HBM per device.

v0:
```python
import jax
import jax.numpy as jnp
from jax import lax
from jax.sharding import PartitionSpec as P

L = 512
SEQS_DEV = 4
STEP = 10
HD = 64
norm_eps = 1e-05
beta_one = 0.9
beta_two = 0.999
learn_rate = 0.02
decay_rate = 0.01
adam_eps = 1e-08


def layer_norm(resid, gain, shift):
    center = resid - jnp.mean(resid, axis=-1, keepdims=True)
    inv_std = lax.rsqrt(jnp.mean(center * center, axis=-1, keepdims=True) + norm_eps)
    normed = center * inv_std
    return (normed * (1.0 + gain) + shift, normed, inv_std)


def norm_back(upstream, normed, inv_std, gain):
    scaled = upstream * (1.0 + gain)
    return inv_std * (
        scaled
        - jnp.mean(scaled, axis=-1, keepdims=True)
        - normed * jnp.mean(scaled * normed, axis=-1, keepdims=True)
    )


def gelu_pair(before):
    cumul = 0.5 * (1.0 + lax.erf(before * 0.7071067811865476))
    density = jnp.exp(-0.5 * before * before) * 0.3989422804014327
    return (before * cumul, cumul + before * density)


def adamw_step(weight, moments, grad, decay):
    first = beta_one * moments[0] + (1.0 - beta_one) * grad
    second = beta_two * moments[1] + (1.0 - beta_two) * grad * grad
    scale_one = 1.0 - beta_one**STEP
    scale_two = 1.0 - beta_two**STEP
    update = first / scale_one / (jnp.sqrt(second / scale_two) + adam_eps) + decay * weight
    return (weight - learn_rate * update, jnp.stack([first, second]))


def live_rows(lengths, count):
    positions = jnp.arange(count, dtype=jnp.int32)
    slot_ids = jnp.arange(lengths.shape[0], dtype=jnp.int32)
    chosen = (positions // L)[:, None] == slot_ids[None, :]
    row_length = jnp.sum(jnp.where(chosen, lengths[None, :], 0), axis=1)
    return positions % L < row_length


def spread(rows_b):
    return lax.all_gather(rows_b, "tensor", axis=0, tiled=True)


def split_heads(matrix, heads_dev):
    return matrix.reshape(SEQS_DEV, L, heads_dev, HD)


def head_scores(query_h, keys_h, key_mask):
    raw = jnp.einsum(
        "sqhe,skhe->shqk", query_h, keys_h, preferred_element_type=jnp.float32
    ) * HD ** (-0.5)
    return jnp.where(key_mask, raw, -jnp.inf)


def on_device(
    block_in,
    cotangent,
    lengths,
    qkv_weight,
    proj_weight,
    expand_weight,
    reduce_weight,
    split_bias,
    vector_params,
    qkv_moments,
    proj_moments,
    expand_moments,
    reduce_moments,
    bias_moments,
    vector_moments,
):
    half = jnp.bfloat16
    single = jnp.float32
    qkv_w, proj_w, expand_w, reduce_w, bias_w, vector_w = (
        lax.all_gather(qkv_weight.astype(half), "dp", axis=1, tiled=True),
        lax.all_gather(proj_weight.astype(half), "dp", axis=1, tiled=True),
        lax.all_gather(expand_weight.astype(half), "dp", axis=0, tiled=True),
        lax.all_gather(reduce_weight.astype(half), "dp", axis=1, tiled=True),
        lax.all_gather(split_bias.astype(half), "dp", axis=1, tiled=True),
        lax.all_gather(vector_params.astype(half), "dp", axis=1, tiled=True),
    )
    heads_dev = bias_w.shape[0]
    width = heads_dev * HD
    bias_f = bias_w.astype(single)
    query_bias = bias_f[:, :HD].reshape(width)
    value_bias = bias_f[:, HD : 2 * HD].reshape(width)
    hidden_bias = bias_f[:, 2 * HD :].reshape(-1)
    vectors = vector_w.astype(single)
    share = block_in.shape[0]
    total_rows = share * lax.axis_size("tensor")
    first_row = lax.axis_index("tensor") * share
    live_full = live_rows(lengths, total_rows)
    key_mask = live_full.reshape(SEQS_DEV, 1, 1, L)
    x_full = spread(block_in)

    def reduce_rows(term):
        return lax.psum(term.astype(jnp.bfloat16), "tensor").astype(jnp.float32)

    def own_rows(matrix):
        return lax.dynamic_slice_in_dim(matrix, first_row, share, 0)

    projected = jnp.einsum("td,jde->jte", x_full, qkv_w, preferred_element_type=single)
    query = (projected[0] + query_bias).astype(half)
    keys = projected[1].astype(half)
    values = (projected[2] + value_bias).astype(half)
    query_h = split_heads(query, heads_dev)
    keys_h = split_heads(keys, heads_dev)
    values_h = split_heads(values, heads_dev)
    scores = head_scores(query_h, keys_h, key_mask)
    row_max = jnp.max(scores, axis=-1, keepdims=True)
    exponent = jnp.exp(scores - row_max)
    denominator = jnp.sum(exponent, axis=-1, keepdims=True)
    log_total = row_max + jnp.log(denominator)
    weights_b = (exponent / denominator).astype(half)
    heads_out = jnp.einsum("shqk,skhe->sqhe", weights_b, values_h, preferred_element_type=single)
    heads_out = heads_out.astype(half).reshape(total_rows, width)
    attn_term = jnp.dot(heads_out, proj_w, preferred_element_type=single)
    resid_one = x_full.astype(single) + reduce_rows(attn_term) + vectors[0]
    hidden_f, normed_one, inv_one = layer_norm(resid_one, vectors[1], vectors[2])
    hidden_b = hidden_f.astype(half)
    before = jnp.dot(hidden_b, expand_w, preferred_element_type=single) + hidden_bias
    active, slope = gelu_pair(before)
    active_b = active.astype(half)
    ffn_term = jnp.dot(active_b, reduce_w, preferred_element_type=single)
    resid_two = hidden_f + reduce_rows(ffn_term) + vectors[3]
    out_f, normed_two, inv_two = layer_norm(resid_two, vectors[4], vectors[5])
    block_out = own_rows(out_f).astype(half)
    grad_out = jnp.where(live_full[:, None], spread(cotangent).astype(single), 0.0)
    d_two = norm_back(grad_out, normed_two, inv_two, vectors[4])
    d_two_b = d_two.astype(half)
    g_reduce = jnp.einsum("tf,td->fd", active_b, d_two_b, preferred_element_type=single)
    d_pre = jnp.einsum("td,fd->tf", d_two_b, reduce_w, preferred_element_type=single) * slope
    g_hidden_bias = jnp.sum(d_pre, axis=0)
    d_pre_b = d_pre.astype(half)
    g_expand = jnp.einsum("td,tf->df", hidden_b, d_pre_b, preferred_element_type=single)
    hidden_term = jnp.einsum("tf,df->td", d_pre_b, expand_w, preferred_element_type=single)
    d_hidden = d_two + reduce_rows(hidden_term)
    d_one = norm_back(d_hidden, normed_one, inv_one, vectors[1])
    vector_parts = jnp.stack(
        [
            jnp.sum(d_one, axis=0),
            jnp.sum(d_hidden * normed_one, axis=0),
            jnp.sum(d_hidden, axis=0),
            jnp.sum(d_two, axis=0),
            jnp.sum(grad_out * normed_two, axis=0),
            jnp.sum(grad_out, axis=0),
        ]
    )
    d_one_b = d_one.astype(half)
    g_proj = jnp.einsum("te,td->ed", heads_out, d_one_b, preferred_element_type=single)
    d_heads = jnp.einsum("td,ed->te", d_one_b, proj_w, preferred_element_type=single).astype(half)
    d_heads_h = split_heads(d_heads, heads_dev)
    back_prob = jnp.exp(head_scores(query_h, keys_h, key_mask) - log_total)
    d_prob = jnp.einsum("sqhe,skhe->shqk", d_heads_h, values_h, preferred_element_type=single)
    delta = jnp.sum(back_prob * d_prob, axis=-1, keepdims=True)
    d_score = (back_prob * (d_prob - delta) * HD ** (-0.5)).astype(half)
    back_b = back_prob.astype(half)
    d_query = jnp.einsum("shqk,skhe->sqhe", d_score, keys_h, preferred_element_type=single)
    d_keys = jnp.einsum("shqk,sqhe->skhe", d_score, query_h, preferred_element_type=single)
    d_values = jnp.einsum("shqk,sqhe->skhe", back_b, d_heads_h, preferred_element_type=single)
    d_query = d_query.reshape(total_rows, width)
    d_keys = d_keys.reshape(total_rows, width)
    d_values = d_values.reshape(total_rows, width)
    d_stack = jnp.stack([d_query, d_keys, d_values]).astype(half)
    g_qkv = jnp.einsum("td,jte->jde", x_full, d_stack, preferred_element_type=single)
    input_term = jnp.einsum("jte,jde->td", d_stack, qkv_w, preferred_element_type=single)
    input_grad = own_rows(d_one + reduce_rows(input_term)).astype(half)
    g_split = jnp.concatenate(
        [
            jnp.sum(d_query, axis=0).reshape(heads_dev, HD),
            jnp.sum(d_values, axis=0).reshape(heads_dev, HD),
            g_hidden_bias.reshape(heads_dev, -1),
        ],
        axis=1,
    )
    qkv_sum, proj_sum, expand_sum, reduce_sum, bias_sum, vector_sum = (
        lax.psum_scatter(g_qkv, "dp", scatter_dimension=1, tiled=True),
        lax.psum_scatter(g_proj, "dp", scatter_dimension=1, tiled=True),
        lax.psum_scatter(g_expand, "dp", scatter_dimension=0, tiled=True),
        lax.psum_scatter(g_reduce, "dp", scatter_dimension=1, tiled=True),
        lax.psum_scatter(g_split, "dp", scatter_dimension=1, tiled=True),
        lax.psum_scatter(vector_parts, "dp", scatter_dimension=1, tiled=True),
    )
    qkv_new, qkv_state = adamw_step(qkv_weight, qkv_moments, qkv_sum, decay_rate)
    proj_new, proj_state = adamw_step(proj_weight, proj_moments, proj_sum, decay_rate)
    expand_new, expand_state = adamw_step(expand_weight, expand_moments, expand_sum, decay_rate)
    reduce_new, reduce_state = adamw_step(reduce_weight, reduce_moments, reduce_sum, decay_rate)
    bias_new, bias_state = adamw_step(split_bias, bias_moments, bias_sum, 0.0)
    vector_new, vector_state = adamw_step(vector_params, vector_moments, vector_sum, 0.0)
    return (
        block_out,
        input_grad,
        qkv_sum,
        proj_sum,
        expand_sum,
        reduce_sum,
        bias_sum,
        vector_sum,
        qkv_new,
        proj_new,
        expand_new,
        reduce_new,
        bias_new,
        vector_new,
        qkv_state,
        proj_state,
        expand_state,
        reduce_state,
        bias_state,
        vector_state,
    )


def solution(mesh):
    placed = (
        P(("dp", "tensor"), None),
        P(("dp", "tensor"), None),
        P("dp"),
        P(None, "dp", "tensor"),
        P("tensor", "dp"),
        P("dp", "tensor"),
        P("tensor", "dp"),
        P("tensor", "dp"),
        P(None, "dp"),
        P(None, None, "dp", "tensor"),
        P(None, "tensor", "dp"),
        P(None, "dp", "tensor"),
        P(None, "tensor", "dp"),
        P(None, "tensor", "dp"),
        P(None, None, "dp"),
    )
    return jax.shard_map(
        on_device,
        mesh=mesh,
        in_specs=placed,
        out_specs=(
            P(("dp", "tensor"), None),
            P(("dp", "tensor"), None),
            P(None, "dp", "tensor"),
            P("tensor", "dp"),
            P("dp", "tensor"),
            P("tensor", "dp"),
            P("tensor", "dp"),
            P(None, "dp"),
            P(None, "dp", "tensor"),
            P("tensor", "dp"),
            P("dp", "tensor"),
            P("tensor", "dp"),
            P("tensor", "dp"),
            P(None, "dp"),
            P(None, None, "dp", "tensor"),
            P(None, "tensor", "dp"),
            P(None, "dp", "tensor"),
            P(None, "tensor", "dp"),
            P(None, "tensor", "dp"),
            P(None, None, "dp"),
        ),
        check_vma=False,
    )
```

profile of v0, /device:TPU:0, one launch (start us, length us, event | category | flops | bytes accessed | tf_op | source)
XLA Modules:
  0.0 728.4 jit_solution(12276453182244348398)
XLA Ops:
  9.5 9.4 %all-gather = bf16[4,96,2]{1,2,0:T(2,128)(2,1)S(1)} all-gather(bf16[1,96,2]{1,2,0:T(2,128)(2,1)S(1)} %convert_bitcast_fusion), channel_id=1, replica_groups=mesh['dp'=4,'tensor'=8] {'dp'}, dimensions={0}, use_global_device_ids=true | all-gather | bytes 1920 | tf_op jit(solution)/shard_map/all_gather | solution.py:96
  22.1 10.0 %all_gather.27 = bf16[128,1024]{1,0:T(8,128)(2,1)S(1)} all-gather(bf16[128,256]{1,0:T(8,128)(2,1)S(1)} %convert_element_type.117), channel_id=1, replica_groups=mesh['dp'=4,'tensor'=8] {'dp'}, dimensions={1}, use_global_device_ids=true | all-gather | bytes 327680 | tf_op jit(solution)/shard_map/all_gather | solution.py:93
  32.0 13.3 %all_gather.25 = bf16[3,1024,128]{1,2,0:T(8,128)(2,1)S(1)} all-gather(bf16[3,256,128]{1,2,0:T(8,128)(2,1)S(1)} %convert_element_type.108), channel_id=1, replica_groups=mesh['dp'=4,'tensor'=8] {'dp'}, dimensions={1}, use_global_device_ids=true | all-gather | bytes 983040 | tf_op jit(solution)/shard_map/all_gather | solution.py:92
  45.4 14.6 %all-gather.6.cloned.1.call-done = bf16[2048,1024]{1,0:T(8,128)(2,1)} async-done(((bf16[256,1024]{1,0:T(8,128)(2,1)}), bf16[2048,1024]{1,0:T(8,128)(2,1)}) %all-gather.6.cloned.1.call-update) | async-done | bytes 4194320 | tf_op jit(solution)/shard_map/all_gather | solution.py:58
  81.2 8.7 %all_gather.28 = bf16[6,1024]{1,0:T(8,128)(2,1)S(1)} all-gather(bf16[6,256]{1,0:T(8,128)(2,1)S(1)} %convert_element_type.120), channel_id=1, replica_groups=mesh['dp'=4,'tensor'=8] {'dp'}, dimensions={1}, use_global_device_ids=true | all-gather | bytes 15360 | tf_op jit(solution)/shard_map/all_gather | solution.py:97
  90.0 85.0 %all-reduce.5.cloned.1.call-done = bf16[2048,1024]{1,0:T(8,128)(2,1)} async-done(((bf16[2048,1024]{1,0:T(8,128)(2,1)}), bf16[2048,1024]{1,0:T(8,128)(2,1)}) %all-reduce.5.cloned.1.call-update) | async-done | bytes 4194320 | tf_op jit(solution)/shard_map/psum | solution.py:114
  175.0 5.0 fusion.7
  183.1 7.5 %multiply_convert_fusion.1 = (bf16[2048,512]{1,0:T(8,128)(2,1)}, f32[2048,512]{1,0:T(8,128)}) fusion(f32[512]{0:T(512)S(1)} %bitcast.225, bf16[1024,512]{1,0:T(8,128)(2,1)} %all-gather.8.cloned.1.call-done, f32[1024]{0:T(1024)S(1)} %bitcast.203, f32[1024]{0:T(1024)S(1)} %bitcast.192, f32[2048]{0:T(1024)S(1)} %add_rsqrt_fusion.1, ...), kind=kOutput, calls=%fused_computation.46 | convolution fusion | flops 2172649472 | bytes 15759360 | tf_op jit(solution)/shard_map/dot_general | solution.py:138
  190.6 6.1 convolution_convert_fusion.1
  197.5 95.9 %all-reduce.7.cloned.1.call-done = bf16[2048,1024]{1,0:T(8,128)(2,1)} async-done(((bf16[2048,1024]{1,0:T(8,128)(2,1)}), bf16[2048,1024]{1,0:T(8,128)(2,1)}) %all-reduce.7.cloned.1.call-update) | async-done | bytes 4194320 | tf_op jit(solution)/shard_map/psum | solution.py:114
  293.4 7.9 %fusion.74 = f32[2048]{0:T(1024)S(1)} fusion(f32[1024]{0:T(1024)S(1)} %bitcast.208, bf16[2048,1024]{1,0:T(8,128)(2,1)} %all-reduce.7.cloned.1.call-done, f32[1024]{0:T(1024)S(1)} %bitcast.204, f32[1024]{0:T(1024)S(1)} %bitcast.193, f32[2048]{0:T(1024)S(1)} %add_rsqrt_fusion.1, f32[2048]{0:T(1024)S(1)} %broadcast_multiply_fusion.5, f32[1024]{0:T(1024)S(1)} %bitcast.186, ...), kind=kLoop, calls=%fused_computation.102 | loop fusion | flops 25163776 | bytes 12623872 | tf_op jit(solution)/shard_map/reduce_sum | solution.py:19
  301.8 5.0 multiply_reduce_fusion.5
  306.8 35.0 %all-gather.12.cloned.1.call-done = bf16[2048,1024]{1,0:T(8,128)(2,1)} async-done(((bf16[256,1024]{1,0:T(8,128)(2,1)}), bf16[2048,1024]{1,0:T(8,128)(2,1)}) %all-gather.12.cloned.1.call-update) | async-done | bytes 4194320 | tf_op jit(solution)/shard_map/all_gather | solution.py:58
  341.8 11.6 %multiply_reduce_fusion = (f32[1024]{0:T(1024)S(1)}, f32[2048]{0:T(1024)S(1)}, f32[2048]{0:T(1024)S(1)}, f32[1024]{0:T(1024)S(1)}, f32[2048,1024]{1,0:T(8,128)S(1)}) fusion(bf16[2048,1024]{1,0:T(8,128)(2,1)} %all-gather.12.cloned.1.call-done, pred[2048]{0:T(1024)(128)(4,1)S(1)} %fusion.98, f32[1024]{0:T(1024)S(1)} %bitcast.200, f32[2048]{0:T(1024)S(1)} %add_rsqrt_fusion, ...), kind=kLoop, calls=%fused_computation.2 | loop fusion | flops 46131200 | bytes 25245696 | tf_op jit(solution)/shard_map/reduce_sum | solution.py:162
  359.8 4.1 fusion.133
  365.3 4.4 convolution_convert_fusion
  370.0 95.1 %all-reduce.9.cloned.1.call-done = bf16[2048,1024]{1,0:T(8,128)(2,1)} async-done(((bf16[2048,1024]{1,0:T(8,128)(2,1)}), bf16[2048,1024]{1,0:T(8,128)(2,1)}) %all-reduce.9.cloned.1.call-update) | async-done | bytes 4194320 | tf_op jit(solution)/shard_map/psum | solution.py:114
  465.1 12.0 %multiply_reduce_fusion.1 = (f32[1024]{0:T(1024)S(1)}, f32[2048]{0:T(1024)S(1)}, f32[2048]{0:T(1024)S(1)}, f32[1024]{0:T(1024)S(1)}, f32[1024]{0:T(1024)S(1)}) fusion(f32[2048,1024]{1,0:T(8,128)} %copy-done.7, bf16[2048,1024]{1,0:T(8,128)(2,1)} %all-reduce.9.cloned.1.call-done, f32[2048]{0:T(1024)S(1)} %add_rsqrt_fusion.1, ...), kind=kLoop, calls=%fused_computation.3 | loop fusion | flops 33547264 | bytes 21024768 | tf_op jit(solution)/shard_map/reduce_sum | solution.py:159
  477.2 6.6 fusion.123
  493.4 6.1 fusion.77
  499.4 6.2 fusion.126
  505.7 16.0 %fusion.125 = (f32[2,64]{1,0:T(2,128)S(1)}, bf16[4,512,2,64]{1,3,2,0:T(8,128)(2,1)S(1)}) fusion(f32[4,2,512,512]{2,3,1,0:T(8,128)} %fusion.77, f32[4,2,512]{2,1,0:T(2,128)S(1)} %bitcast.223, f32[4,2,512,512]{2,3,1,0:T(8,128)} %copy-done.8, pred[4,512]{1,0:T(4,128)(4,1)S(1)} %fusion.96, bf16[4,512,2,64]{1,0,3,2:T(4,128)(2,1)S(1)} %convert_element_type.113), kind=kOutput, calls=%fused_computation.184 | convolution fusion | flops 292032896 | bytes 17844736 | tf_op jit(solution)/shard_map/shqk,skhe->sqhe/dot_general | solution.py:175
  522.6 4.9 fusion.34
  528.2 15.8 %fusion.53 = bf16[4,512,2,64]{1,3,2,0:T(8,128)(2,1)S(1)} fusion(f32[4,2,512,512]{2,3,1,0:T(8,128)} %fusion.77, f32[4,2,512]{2,1,0:T(2,128)S(1)} %bitcast.224, f32[4,2,512,512]{2,3,1,0:T(8,128)} %copy-done.8, pred[4,512]{1,0:T(4,128)(4,1)S(1)} %fusion.96, f32[4,512,2,64]{1,0,3,2:T(4,128)S(1)} %squeeze.5, f32[2,64]{1,0:T(2,128)S(1)} %get-tuple-element.167), kind=kOutput, calls=%fused_computation.67 | convolution fusion | flops 292295168 | bytes 18369024 | tf_op jit(solution)/shard_map/shqk,sqhe->skhe/dot_general | solution.py:176
  548.1 5.0 bitcast_convert_fusion
  553.1 8.6 %fusion.57 = f32[1024,512]{1,0:T(8,128)} fusion(f32[1024]{0:T(1024)S(1)} %bitcast.207, f32[1024]{0:T(1024)S(1)} %bitcast.198, bf16[2048,512]{1,0:T(8,128)(2,1)} %copy-done.34, bf16[2048,1024]{1,0:T(8,128)(2,1)} %all-reduce.5.cloned.1.call-done, bf16[2048,1024]{1,0:T(8,128)(2,1)} %all-gather.6.cloned.1.call-done, f32[2048]{0:T(1024)S(1)} %add_rsqrt_fusion.1, ...), kind=kOutput, calls=%fused_computation.69 | convolution fusion | flops 2166358016 | bytes 12611584 | tf_op jit(solution)/shard_map/td,tf->df/dot_general | solution.py:152
  562.1 7.8 %fusion.37 = f32[512,1024]{1,0:T(8,128)} fusion(bf16[2048,512]{1,0:T(8,128)(2,1)} %get-tuple-element.170, f32[2048,1024]{1,0:T(8,128)} %copy-done.7), kind=kOutput, calls=%fused_computation.59 | convolution fusion | flops 2149580800 | bytes 12582912 | tf_op jit(solution)/shard_map/tf,td->fd/dot_general | solution.py:148
  570.0 5.3 fusion.40
  582.0 22.0 %reduce-scatter.11.cloned.1.call-done = f32[128,256]{1,0:T(8,128)} async-done(((f32[128,1024]{1,0:T(8,128)}), f32[128,256]{1,0:T(8,128)}) %reduce-scatter.11.cloned.1.call-update) | async-done | bytes 131088 | tf_op jit(solution)/shard_map/reduce_scatter | solution.py:195
  606.4 43.4 %all-reduce.11.cloned.1.call-done = bf16[2048,1024]{1,0:T(8,128)(2,1)} async-done(((bf16[2048,1024]{1,0:T(8,128)(2,1)}), bf16[2048,1024]{1,0:T(8,128)(2,1)}) %all-reduce.11.cloned.1.call-update) | async-done | bytes 4194320 | tf_op jit(solution)/shard_map/psum | solution.py:114
  655.9 25.3 %reduce-scatter.15.cloned.1.call-done = f32[512,256]{1,0:T(8,128)} async-done(((f32[512,1024]{1,0:T(8,128)}), f32[512,256]{1,0:T(8,128)}) %reduce-scatter.15.cloned.1.call-update) | async-done | bytes 524304 | tf_op jit(solution)/shard_map/reduce_scatter | solution.py:197
  684.8 30.3 %reduce-scatter.9.cloned.1.call-done = f32[3,256,128]{1,2,0:T(8,128)} async-done(((f32[3,1024,128]{1,2,0:T(8,128)}), f32[3,256,128]{1,2,0:T(8,128)}) %reduce-scatter.9.cloned.1.call-update) | async-done | bytes 393232 | tf_op jit(solution)/shard_map/reduce_scatter | solution.py:194
  (184 shorter events, 77.9 us)
Async XLA Ops:
  8.0 52.0 %all-gather.6.cloned.1.call-start = ((), (), s32[]{:S(2)}) async-start(), calls=%async_computation.6 | async-start | bytes 4718592 | tf_op jit(solution)/shard_map/all_gather | solution.py:58
  8.8 166.2 %all-reduce.5.cloned.1.call-start = ((), (), s32[]{:S(2)}) async-start(), calls=%async_computation.7 | async-start | bytes 8388608 | tf_op jit(solution)/shard_map/psum | solution.py:114
  21.0 44.3 %copy-start.14 = (f32[3,256,128]{1,2,0:T(8,128)}, f32[3,256,128]{1,2,0:T(8,128)S(1)}, u32[]{:S(2)}) copy-start(f32[3,256,128]{1,2,0:T(8,128)S(1)} %copy.154) | copy-start | bytes 1179652
  45.3 14.7 %copy-start.22 = (bf16[3,1024,128]{1,2,0:T(8,128)(2,1)}, bf16[3,1024,128]{1,2,0:T(8,128)(2,1)S(1)}, u32[]{:S(2)}) copy-start(bf16[3,1024,128]{1,2,0:T(8,128)(2,1)S(1)} %all_gather.25) | copy-start | bytes 2359300
  79.5 103.5 %all-gather.8.cloned.1.call-start = ((), (), s32[]{:S(2)}) async-start(), calls=%async_computation.8 | async-start | bytes 1310720 | tf_op jit(solution)/shard_map/all_gather | solution.py:94
  80.4 110.2 %all-gather.10.cloned.1.call-start = ((), (), s32[]{:S(2)}) async-start(), calls=%async_computation.9 | async-start | bytes 1310720 | tf_op jit(solution)/shard_map/all_gather | solution.py:95
  81.2 212.2 %all-reduce.7.cloned.1.call-start = ((), (), s32[]{:S(2)}) async-start(), calls=%async_computation.10 | async-start | bytes 8388608 | tf_op jit(solution)/shard_map/psum | solution.py:114
  196.7 145.1 %all-gather.12.cloned.1.call-start = ((), (), s32[]{:S(2)}) async-start(), calls=%async_computation.11 | async-start | bytes 4718592 | tf_op jit(solution)/shard_map/all_gather | solution.py:58
  197.3 267.8 %all-reduce.9.cloned.1.call-start = ((), (), s32[]{:S(2)}) async-start(), calls=%async_computation.12 | async-start | bytes 8388608 | tf_op jit(solution)/shard_map/psum | solution.py:114
  293.4 7.9 %copy-start.1 = (bf16[2048,1024]{1,0:T(8,128)(2,1)S(1)}, bf16[2048,1024]{1,0:T(8,128)(2,1)}, u32[]{:S(2)}) copy-start(bf16[2048,1024]{1,0:T(8,128)(2,1)} %all-gather.6.cloned.1.call-done) | copy-start | bytes 12582916
  293.4 7.9 %copy-start.4 = (bf16[2048,1024]{1,0:T(8,128)(2,1)S(1)}, bf16[2048,1024]{1,0:T(8,128)(2,1)}, u32[]{:S(2)}) copy-start(bf16[2048,1024]{1,0:T(8,128)(2,1)} %all-reduce.5.cloned.1.call-done) | copy-start | bytes 12582916
  293.4 8.4 %copy-start.10 = (bf16[2048,1024]{1,0:T(8,128)(2,1)S(1)}, bf16[2048,1024]{1,0:T(8,128)(2,1)}, u32[]{:S(2)}) copy-start(bf16[2048,1024]{1,0:T(8,128)(2,1)} %all-reduce.7.cloned.1.call-done) | copy-start | bytes 12582916
  341.8 11.7 %copy-start.11 = (bf16[2048,1024]{1,0:T(8,128)(2,1)S(1)}, bf16[2048,1024]{1,0:T(8,128)(2,1)}, u32[]{:S(2)}) copy-start(bf16[2048,1024]{1,0:T(8,128)(2,1)} %all-gather.12.cloned.1.call-done) | copy-start | bytes 12582916
  369.7 208.3 %reduce-scatter.19.cloned.1.call-start = ((), (), s32[]{:S(2)}) async-start(), calls=%async_computation.19 | async-start | bytes 245760
  465.1 12.0 %copy-start.2 = (bf16[2048,1024]{1,0:T(8,128)(2,1)S(1)}, bf16[2048,1024]{1,0:T(8,128)(2,1)}, u32[]{:S(2)}) copy-start(bf16[2048,1024]{1,0:T(8,128)(2,1)} %all-gather.6.cloned.1.call-done) | copy-start | bytes 12582916
  465.1 12.0 %copy-start.5 = (bf16[2048,1024]{1,0:T(8,128)(2,1)S(1)}, bf16[2048,1024]{1,0:T(8,128)(2,1)}, u32[]{:S(2)}) copy-start(bf16[2048,1024]{1,0:T(8,128)(2,1)} %all-reduce.5.cloned.1.call-done) | copy-start | bytes 12582916
  465.1 12.0 %copy-start.12 = (bf16[2048,1024]{1,0:T(8,128)(2,1)S(1)}, bf16[2048,1024]{1,0:T(8,128)(2,1)}, u32[]{:S(2)}) copy-start(bf16[2048,1024]{1,0:T(8,128)(2,1)} %all-reduce.9.cloned.1.call-done) | copy-start | bytes 12582916
  522.6 57.5 %reduce-scatter.17.cloned.1.call-start = ((), (), s32[]{:S(2)}) async-start(), calls=%async_computation.18 | async-start | bytes 40960 | tf_op jit(solution)/shard_map/reduce_scatter | solution.py:199
  528.2 18.4 %copy-start.23 = (bf16[4,512,2,64]{1,3,2,0:T(8,128)(2,1)S(1)}, bf16[4,512,2,64]{1,3,2,0:T(8,128)(2,1)}, u32[]{:S(2)}) copy-start(bf16[4,512,2,64]{1,3,2,0:T(8,128)(2,1)} %get-tuple-element.143) | copy-start | bytes 1572868
  528.2 75.8 %reduce-scatter.11.cloned.1.call-start = ((), (), s32[]{:S(2)}) async-start(), calls=%async_computation.15 | async-start | bytes 655360 | tf_op jit(solution)/shard_map/reduce_scatter | solution.py:195
  547.8 101.9 %all-reduce.11.cloned.1.call-start = ((), (), s32[]{:S(2)}) async-start(), calls=%async_computation.13 | async-start | bytes 8388608 | tf_op jit(solution)/shard_map/psum | solution.py:114
  553.1 99.0 %reduce-scatter.13.cloned.1.call-start = ((), (), s32[]{:S(2)}) async-start(), calls=%async_computation.16 | async-start | bytes 2621440 | tf_op jit(solution)/shard_map/reduce_scatter | solution.py:196
  561.7 119.4 %reduce-scatter.15.cloned.1.call-start = ((), (), s32[]{:S(2)}) async-start(), calls=%async_computation.17 | async-start | bytes 2621440 | tf_op jit(solution)/shard_map/reduce_scatter | solution.py:197
  569.9 9.0 %copy-start.29 = (f32[2,2,96]{2,1,0:T(2,128)S(1)}, f32[2,2,96]{2,1,0:T(2,128)}, u32[]{:S(2)}) copy-start(f32[2,2,96]{2,1,0:T(2,128)} %param.28) | copy-start | bytes 4612
  569.9 9.0 %copy-start.30 = (f32[2,96]{1,0:T(2,128)S(1)}, f32[2,96]{1,0:T(2,128)}, u32[]{:S(2)}) copy-start(f32[2,96]{1,0:T(2,128)} %param.22) | copy-start | bytes 2308
  569.9 34.1 %copy-start.24 = (f32[128,256]{1,0:T(8,128)S(1)}, f32[128,256]{1,0:T(8,128)}, u32[]{:S(2)}) copy-start(f32[128,256]{1,0:T(8,128)} %param.19) | copy-start | bytes 393220
  569.9 34.1 %copy-start.25 = (f32[2,128,256]{2,1,0:T(8,128)S(1)}, f32[2,128,256]{2,1,0:T(8,128)}, u32[]{:S(2)}) copy-start(f32[2,128,256]{2,1,0:T(8,128)} %param.25) | copy-start | bytes 786436
  570.0 82.1 %copy-start.17 = (f32[256,512]{1,0:T(8,128)S(1)}, f32[256,512]{1,0:T(8,128)}, u32[]{:S(2)}) copy-start(f32[256,512]{1,0:T(8,128)} %param.20) | copy-start | bytes 1572868
  570.0 145.1 %reduce-scatter.9.cloned.1.call-start = ((), (), s32[]{:S(2)}) async-start(), calls=%async_computation.14 | async-start | bytes 1966080 | tf_op jit(solution)/shard_map/reduce_scatter | solution.py:194
  575.3 105.9 %copy-start.19 = (f32[512,256]{1,0:T(8,128)S(1)}, f32[512,256]{1,0:T(8,128)}, u32[]{:S(2)}) copy-start(f32[512,256]{1,0:T(8,128)} %param.21) | copy-start | bytes 1572868
  575.8 139.3 %copy-start.15 = (f32[3,256,128]{1,2,0:T(8,128)S(1)}, f32[3,256,128]{1,2,0:T(8,128)}, u32[]{:S(2)}) copy-start(f32[3,256,128]{1,2,0:T(8,128)} %copy-done.14) | copy-start | bytes 1179652
  578.9 137.5 %copy-start.28 = (f32[2,96]{1,0:T(2,128)}, f32[2,96]{1,0:T(2,128)S(1)}, u32[]{:S(2)}) copy-start(f32[2,96]{1,0:T(2,128)S(1)} %copy.196) | copy-start | bytes 2308
  (17 other events, 81.3 us)
Sparse Core Ops, SparseCore 0:
  10.4 49.5 all-gather.5
  79.7 95.2 all-reduce.4
  196.8 96.5 all-reduce.6
  294.9 46.9 all-gather.11
  369.8 95.2 all-reduce.8
  553.2 96.5 all-reduce.10
Sparse Core Ops, SparseCore 1:
  82.4 25.2 all-gather.7
  109.9 26.2 all-gather.9
  522.6 24.3 reduce-scatter.18
  550.9 24.0 reduce-scatter.16
  578.9 25.0 reduce-scatter.10
  607.6 35.0 reduce-scatter.12
  646.1 35.1 reduce-scatter.14
  684.0 31.0 reduce-scatter.8
where the time goes:
time: 737 us; the launch traced here: 728 us
  waiting for transfers between devices  448 us (61%)
  matrix products  111 us (15%)
  other arithmetic  77.2 us (10%)
  blocking collectives  41.4 us (6%)
  local copies, waits for them, and re-layouts  32.2 us (4%)
  between operations  16.9 us (2%)
    psum x4, waiting for transfers between devices, reduce_rows(): return lax.psum(term.astype(jnp.bfloat16), 'tensor').astype(jnp.float32)  319 us
    all_gather x2, waiting for transfers between devices, spread(): return lax.all_gather(rows_b, 'tensor', axis=0, tiled=True)  49.6 us
    reduce_scatter x1, waiting for transfers between devices, on_device(): lax.psum_scatter(g_qkv, 'dp', scatter_dimension=1, tiled=True)  30.3 us
    reduce_scatter x1, waiting for transfers between devices, on_device(): lax.psum_scatter(g_reduce, 'dp', scatter_dimension=1, tiled=True)  25.3 us
    reduce_scatter x1, waiting for transfers between devices, on_device(): lax.psum_scatter(g_proj, 'dp', scatter_dimension=1, tiled=True)  22 us
    unnamed x84, local copies, waits for them, and re-layouts  17.6 us
    dot_general x1, matrix products, on_device(): jnp.einsum('shqk,skhe->sqhe', d_score, keys_h, preferred_element_type=sin...  16 us
    dot_general x1, matrix products, on_device(): jnp.einsum('shqk,sqhe->skhe', d_score, query_h, preferred_element_type=si...  15.8 us
  transfers between devices with their start and end apart: 14, of which 9 were waited for; matrix products, arithmetic and copies ran while one was open for 14% of the time, Pallas kernels for 0%

commit v1 on v0

--- a/solution.py
+++ b/solution.py
@@ -111,7 +111,9 @@
     x_full = spread(block_in)
 
     def reduce_rows(term):
-        return lax.psum(term.astype(jnp.bfloat16), "tensor").astype(jnp.float32)
+        return jnp.sum(lax.all_gather(term.astype(jnp.bfloat16), "tensor"), axis=0).astype(
+            jnp.float32
+        )
 
     def own_rows(matrix):
         return lax.dynamic_slice_in_dim(matrix, first_row, share, 0)

time: 737 us -> 1590 us (2.16)
  waiting for transfers between devices: 448 us -> 1250 us
  other arithmetic: 77.2 us -> 136 us
    all_gather x0 -> x4, waiting for transfers between devices: none -> 1120 us  [reduce_rows(): lax.all_gather(term.astype(jnp.bfloat16), 'tensor')]
    psum x4 -> x0, waiting for transfers between devices: 319 us -> none  [reduce_rows(): return lax.psum(term.astype(jnp.bfloat16), 'tensor').astype(jnp.float32)]
    reduce_sum x0 -> x4, other arithmetic: none -> 57.8 us  [reduce_rows(): jnp.sum(lax.all_gather(term.astype(jnp.bfloat16), 'tensor'), axis=0)]
    reduce_scatter x1, waiting for transfers between devices: 25.3 us -> 0.01 us  [on_device(): lax.psum_scatter(g_reduce, 'dp', scatter_dimension=1, tiled=True)]
    all_gather x1, waiting for transfers between devices: 0.01 us -> 21.2 us  [on_device(): lax.all_gather(reduce_weight.astype(half), 'dp', axis=1, tiled=True)]
    all_gather x2, waiting for transfers between devices: 49.6 us -> 32.8 us  [spread(): return lax.all_gather(rows_b, 'tensor', axis=0, tiled=True)]
  transfers between devices with their start and end apart: 14 -> 14, of which waited for: 9 -> 11; matrix products, arithmetic and copies ran while one was open for 14% -> 13% of each run, Pallas kernels for 0% -> 0%
where the time goes in v1:
time: 1590 us; the launch traced here: 1580 us
  waiting for transfers between devices  1250 us (79%)
  other arithmetic  136 us (9%)
  matrix products  114 us (7%)
  blocking collectives  41 us (3%)
  local copies, waits for them, and re-layouts  31.7 us (2%)
    all_gather x4, waiting for transfers between devices, reduce_rows(): lax.all_gather(term.astype(jnp.bfloat16), 'tensor')  1120 us
    reduce_sum x4, other arithmetic, reduce_rows(): jnp.sum(lax.all_gather(term.astype(jnp.bfloat16), 'tensor'), axis=0)  57.8 us
    all_gather x2, waiting for transfers between devices, spread(): return lax.all_gather(rows_b, 'tensor', axis=0, tiled=True)  32.8 us
  transfers between devices with their start and end apart: 14, of which 11 were waited for; matrix products, arithmetic and copies ran while one was open for 13% of the time, Pallas kernels for 0%

profile of v1, /device:TPU:0, one launch (start us, length us, event | category | flops | bytes accessed | tf_op | source)
XLA Modules:
  0.0 1584.9 jit_solution(3031992312584449854)
XLA Ops:
  8.7 9.4 all-gather.4
  21.2 10.0 all_gather.51
  31.2 13.3 all_gather.49
  44.6 14.6 all-gather.14.cloned.1.call-done
  79.1 8.4 all_gather.54
  88.1 276.9 %all-gather.22.cloned.1.call-done = bf16[16384,1024]{1,0:T(8,128)(2,1)} async-done(((bf16[2048,1024]{1,0:T(8,128)(2,1)}), bf16[16384,1024]{1,0:T(8,128)(2,1)}) %all-gather.22.cloned.1.call-update) | async-done | bytes 33554448 | tf_op jit(solution)/shard_map/all_gather | solution.py:114
  365.0 14.4 reduce_sum.233
  392.1 7.5 multiply_convert_fusion.1
  399.6 21.2 %all-gather.18.cloned.1.call-done = bf16[512,1024]{1,0:T(8,128)(2,1)} async-done(((bf16[512,256]{1,0:T(8,128)(2,1)}), bf16[512,1024]{1,0:T(8,128)(2,1)}) %all-gather.18.cloned.1.call-update) | async-done | bytes 1048592 | tf_op jit(solution)/shard_map/all_gather | solution.py:95
  420.7 6.2 convolution_convert_fusion.1
  428.0 287.7 %all-gather.24.cloned.1.call-done = bf16[16384,1024]{1,0:T(8,128)(2,1)} async-done(((bf16[2048,1024]{1,0:T(8,128)(2,1)}), bf16[16384,1024]{1,0:T(8,128)(2,1)}) %all-gather.24.cloned.1.call-update) | async-done | bytes 33554448 | tf_op jit(solution)/shard_map/all_gather | solution.py:114
  715.7 14.8 reduce_sum.236
  730.5 7.8 fusion.74
  744.1 18.2 %all-gather.20.cloned.1.call-done = bf16[2048,1024]{1,0:T(8,128)(2,1)} async-done(((bf16[256,1024]{1,0:T(8,128)(2,1)}), bf16[2048,1024]{1,0:T(8,128)(2,1)}) %all-gather.20.cloned.1.call-update) | async-done | bytes 4194320 | tf_op jit(solution)/shard_map/all_gather | solution.py:58
  762.2 11.6 multiply_reduce_fusion
  790.1 8.6 fusion.57
  798.8 9.4 fusion.37
  808.5 269.1 %all-gather.26.cloned.1.call-done = bf16[16384,1024]{1,0:T(8,128)(2,1)} async-done(((bf16[2048,1024]{1,0:T(8,128)(2,1)}), bf16[16384,1024]{1,0:T(8,128)(2,1)}) %all-gather.26.cloned.1.call-update) | async-done | bytes 33554448 | tf_op jit(solution)/shard_map/all_gather | solution.py:114
  1077.6 14.4 reduce_sum.241
  1092.1 12.2 multiply_reduce_fusion.1
  1104.3 6.7 fusion.123
  1120.7 5.7 fusion.77
  1126.4 16.5 %fusion.125 = (f32[2,64]{1,0:T(2,128)S(1)}, bf16[4,512,2,64]{1,3,2,0:T(8,128)(2,1)}) fusion(f32[4,2,512,512]{2,3,1,0:T(8,128)} %fusion.77, f32[4,2,512]{2,1,0:T(2,128)S(1)} %bitcast.230, f32[4,2,512,512]{2,3,1,0:T(8,128)} %copy-done.9, pred[4,512]{1,0:T(4,128)(4,1)S(1)} %fusion.96, bf16[4,512,2,64]{1,0,3,2:T(4,128)(2,1)S(1)} %copy-done.17), kind=kOutput, calls=%fused_computation.184 | convolution fusion | flops 292032896 | bytes 17844736 | tf_op jit(solution)/shard_map/shqk,skhe->sqhe/dot_general | solution.py:177
  1142.9 6.0 fusion.126
  1155.6 15.7 fusion.53
  1175.4 5.2 fusion.40
  1180.7 5.3 bitcast_convert_fusion
  1199.4 9.4 reduce-scatter.17.cloned.1.call-done
  1210.7 26.4 %reduce-scatter.11.cloned.1.call-done = f32[128,256]{1,0:T(8,128)} async-done(((f32[128,1024]{1,0:T(8,128)}), f32[128,256]{1,0:T(8,128)}) %reduce-scatter.11.cloned.1.call-update) | async-done | bytes 131088 | tf_op jit(solution)/shard_map/reduce_scatter | solution.py:197
  1239.6 31.7 %reduce-scatter.9.cloned.1.call-done = f32[3,256,128]{1,2,0:T(8,128)} async-done(((f32[3,1024,128]{1,2,0:T(8,128)}), f32[3,256,128]{1,2,0:T(8,128)}) %reduce-scatter.9.cloned.1.call-update) | async-done | bytes 393232 | tf_op jit(solution)/shard_map/reduce_scatter | solution.py:196
  1276.7 284.7 %all-gather.28.cloned.1.call-done = bf16[16384,1024]{1,0:T(8,128)(2,1)} async-done(((bf16[2048,1024]{1,0:T(8,128)(2,1)}), bf16[16384,1024]{1,0:T(8,128)(2,1)}) %all-gather.28.cloned.1.call-update) | async-done | bytes 33554448 | tf_op jit(solution)/shard_map/all_gather | solution.py:114
  1561.4 14.2 reduce_sum.245
  (194 shorter events, 106.7 us)
Async XLA Ops:
  7.2 52.0 %all-gather.14.cloned.1.call-start = ((), (), s32[]{:S(2)}) async-start(), calls=%async_computation.6 | async-start | bytes 4718592 | tf_op jit(solution)/shard_map/all_gather | solution.py:58
  7.9 357.0 %all-gather.22.cloned.1.call-start = ((), (), s32[]{:S(2)}) async-start(), calls=%async_computation.15 | async-start | bytes 37748736 | tf_op jit(solution)/shard_map/all_gather | solution.py:114
  20.1 43.4 %copy-start.15 = (f32[3,256,128]{1,2,0:T(8,128)}, f32[3,256,128]{1,2,0:T(8,128)S(1)}, u32[]{:S(2)}) copy-start(f32[3,256,128]{1,2,0:T(8,128)S(1)} %copy.154) | copy-start | bytes 1179652
  44.5 14.7 copy-start.24
  44.6 21.6 %copy-start.31 = (f32[2,64]{1,0:T(2,128)}, f32[2,64]{1,0:T(2,128)S(1)}, u32[]{:S(2)}) copy-start(f32[2,64]{1,0:T(2,128)S(1)} %get-tuple-element.167) | copy-start | bytes 1540
  77.4 314.7 %all-gather.16.cloned.1.call-start = ((), (), s32[]{:S(2)}) async-start(), calls=%async_computation.7 | async-start | bytes 1310720 | tf_op jit(solution)/shard_map/all_gather | solution.py:94
  78.2 342.5 %all-gather.18.cloned.1.call-start = ((), (), s32[]{:S(2)}) async-start(), calls=%async_computation.8 | async-start | bytes 1310720 | tf_op jit(solution)/shard_map/all_gather | solution.py:95
  79.0 636.7 %all-gather.24.cloned.1.call-start = ((), (), s32[]{:S(2)}) async-start(), calls=%async_computation.16 | async-start | bytes 37748736 | tf_op jit(solution)/shard_map/all_gather | solution.py:114
  426.9 335.3 %all-gather.20.cloned.1.call-start = ((), (), s32[]{:S(2)}) async-start(), calls=%async_computation.9 | async-start | bytes 4718592 | tf_op jit(solution)/shard_map/all_gather | solution.py:58
  427.5 650.1 %all-gather.26.cloned.1.call-start = ((), (), s32[]{:S(2)}) async-start(), calls=%async_computation.17 | async-start | bytes 37748736 | tf_op jit(solution)/shard_map/all_gather | solution.py:114
  762.2 11.6 copy-start.12
  790.0 399.4 %reduce-scatter.13.cloned.1.call-start = ((), (), s32[]{:S(2)}) async-start(), calls=%async_computation.12 | async-start | bytes 2621440 | tf_op jit(solution)/shard_map/reduce_scatter | solution.py:198
  798.8 394.3 %reduce-scatter.15.cloned.1.call-start = ((), (), s32[]{:S(2)}) async-start(), calls=%async_computation.13 | async-start | bytes 2621440 | tf_op jit(solution)/shard_map/reduce_scatter | solution.py:199
  808.3 388.4 %reduce-scatter.19.cloned.1.call-start = ((), (), s32[]{:S(2)}) async-start(), calls=%async_computation.19 | async-start | bytes 245760
  1092.1 12.2 copy-start.2
  1092.1 12.2 copy-start.5
  1092.1 12.2 copy-start.11
  1116.3 10.0 copy-start.17
  1126.4 16.5 %copy-start.22 = (bf16[4,512,2,64]{1,3,2,0:T(8,128)(2,1)S(1)}, bf16[4,512,2,64]{1,3,2,0:T(8,128)(2,1)}, u32[]{:S(2)}) copy-start(bf16[4,512,2,64]{1,3,2,0:T(8,128)(2,1)} %copy.162) | copy-start | bytes 1572868
  1142.9 12.7 copy-start.14
  1142.9 12.7 copy-start.32
  1149.8 59.0 %reduce-scatter.17.cloned.1.call-start = ((), (), s32[]{:S(2)}) async-start(), calls=%async_computation.14 | async-start | bytes 40960 | tf_op jit(solution)/shard_map/reduce_scatter | solution.py:201
  1155.5 15.8 copy-start.25
  1155.5 81.6 %reduce-scatter.11.cloned.1.call-start = ((), (), s32[]{:S(2)}) async-start(), calls=%async_computation.11 | async-start | bytes 655360 | tf_op jit(solution)/shard_map/reduce_scatter | solution.py:197
  1175.1 96.2 %reduce-scatter.9.cloned.1.call-start = ((), (), s32[]{:S(2)}) async-start(), calls=%async_computation.10 | async-start | bytes 1966080 | tf_op jit(solution)/shard_map/reduce_scatter | solution.py:196
  1180.6 8.8 copy-start.19
  1180.6 380.8 %all-gather.28.cloned.1.call-start = ((), (), s32[]{:S(2)}) async-start(), calls=%async_computation.18 | async-start | bytes 37748736 | tf_op jit(solution)/shard_map/all_gather | solution.py:114
  1186.0 22.8 %copy-start.29 = (f32[6,256]{1,0:T(8,128)S(1)}, f32[6,256]{1,0:T(8,128)}, u32[]{:S(2)}) copy-start(f32[6,256]{1,0:T(8,128)} %param.23) | copy-start | bytes 18436
  1186.0 51.2 %copy-start.26 = (f32[128,256]{1,0:T(8,128)S(1)}, f32[128,256]{1,0:T(8,128)}, u32[]{:S(2)}) copy-start(f32[128,256]{1,0:T(8,128)} %param.19) | copy-start | bytes 393220
  1186.0 51.1 %copy-start.27 = (f32[2,128,256]{2,1,0:T(8,128)S(1)}, f32[2,128,256]{2,1,0:T(8,128)}, u32[]{:S(2)}) copy-start(f32[2,128,256]{2,1,0:T(8,128)} %param.25) | copy-start | bytes 786436
  1186.1 85.2 %copy-start.16 = (f32[3,256,128]{1,2,0:T(8,128)S(1)}, f32[3,256,128]{1,2,0:T(8,128)}, u32[]{:S(2)}) copy-start(f32[3,256,128]{1,2,0:T(8,128)} %copy-done.15) | copy-start | bytes 1179652
  1197.5 378.1 %copy-start.33 = (f32[2,96]{1,0:T(2,128)}, f32[2,96]{1,0:T(2,128)S(1)}, u32[]{:S(2)}) copy-start(f32[2,96]{1,0:T(2,128)S(1)} %copy.196) | copy-start | bytes 2308
  (20 other events, 107.2 us)
Sparse Core Ops, SparseCore 0:
  9.6 49.5 all-gather.13
  77.5 287.3 all-gather.21
  367.4 24.6 all-gather.15
  394.3 26.3 all-gather.17
  427.0 288.5 all-gather.23
  717.1 45.0 all-gather.19
  790.2 287.4 all-gather.25
  1081.2 33.3 reduce-scatter.12
  1118.1 35.1 reduce-scatter.14
  1156.5 24.2 reduce-scatter.18
  1184.7 24.0 reduce-scatter.16
  1212.0 25.0 reduce-scatter.10
  1240.1 31.0 reduce-scatter.8
  1272.7 288.6 all-gather.27
